TPU v7x, 32 devices: a whole 2x2x4 slice. The times are simulated.
32 devices in a mesh: tile: 8 (over z, y), rad: 4 (over x, core).
Axes of the slice: x: 2, y: 2, z: 4, core: 2. Of those that a mesh axis runs over, the one named last changes fastest.
Arguments:
- fields: float32 [8, 96, 64, 256], P(None, 'rad', 'tile'), may hold values from -6 to 6
- opacity: float32 [96, 64, 256], P('rad', 'tile'), may hold values from 0.0026041667 to 0.041666668
- donor_row: int32 [2048], P('tile'), may hold values from 0 to 4
- donor_column: int32 [2048], P('tile'), may hold values from 0 to 252
- target_tile: int32 [2048, 1], P('tile'), may hold values from 0 to 7; in each aligned block of 256 rows (0 to 255, 256 to 511, ...) at most 64 rows name the same one
- target_cell: int32 [2048], P('tile'), may hold values from 0 to 2047
- lagrange: float32 [16, 2048], P(None, 'tile'), may hold values from -0.2 to 0.5
Outputs:
- updated: float32 [8, 96, 64, 256], P(None, 'rad', 'tile')
Inputs may be any that keep to these rules, and one draw needn't show every extreme that they name: `target_tile`: within the 256 donor points of one tile no target tile appears more than 64 times, and some target tile appears exactly 64 times.
All inputs are finite; a program needn't handle non-finite values.
Results may differ from a plain program's by a relative error of at most 0.00005.
Values sent between devices are 32-bit elements; how exact they have to be, the bound alone decides.
A program may use at most 64 MiB of HBM per device.

v0:
```python
import functools

import jax
import jax.numpy as jnp
from jax import lax
from jax.experimental import pallas as pl
from jax.experimental.pallas import tpu as pltpu
from jax.sharding import PartitionSpec as P

VISCOSITY = 0.1
COUPLING = 1.0
COOL_RATE = 2.0
TIME_STEP = 0.2
MESH = pl.DeviceIdType.MESH
LANES = 128
STEP = 4
EARLY = 2
NT = (((1,), (1,)), ((), ()))


def dot(a, b):
    return jnp.dot(a, b, preferred_element_type=jnp.float32)


def split(x):
    high = x.astype(jnp.bfloat16)
    low = (x - high.astype(jnp.float32)).astype(jnp.bfloat16)
    return high, low


def pair_terms(u, ups, downs):
    s1, s2, s3 = [a + b for a, b in zip(ups, downs)]
    d1, d2, d3 = [a - b for a, b in zip(ups, downs)]
    first = (45.0 / 60.0) * d1 - (9.0 / 60.0) * d2 + (1.0 / 60.0) * d3
    second = (
        (270.0 / 180.0) * s1 - (27.0 / 180.0) * s2 + (2.0 / 180.0) * s3 - (490.0 / 180.0) * u
    )
    return first, second


def kernel(
    n_tile, n_rad, inner, cap,
    f4, f2, opacity, drow, dcol, ttile, tcell, lagrange,
    out,
    x2, ext, acc, psend, precv, relay, ghost, hits, chunks, inc, xall, opsum, oprecv,
    x2_sem, in_sem, lvl_send, lvl_recv, row_send, row_recv, hop_recv, fwd_send, op_send, op_recv,
    a2a_send, a2a_recv, out_sem,
):
    F, L, R, C = acc.shape
    V = F * L
    T = drow.shape[1]
    pack = LANES // cap
    VP = V // pack
    tile = lax.axis_index("tile")
    rad = lax.axis_index("rad")
    quarter = n_tile // 4

    halves = C // LANES
    load_x2 = [
        pltpu.make_async_copy(f2.at[:, pl.ds(h * LANES, LANES)], x2.at[h], x2_sem.at[h])
        for h in range(halves)
    ]
    load_ext = pltpu.make_async_copy(f4, ext.at[:, pl.ds(3, L)], in_sem)
    for copy in load_x2:
        copy.start()
    load_ext.start()

    barrier = pltpu.get_barrier_semaphore()
    for d in range(1, n_tile):
        pl.semaphore_signal(
            barrier, inc=1, device_id=(lax.rem(tile + d, n_tile), rad), device_id_type=MESH
        )
    for d in range(1, n_rad):
        pl.semaphore_signal(
            barrier, inc=1, device_id=(tile, lax.rem(rad + d, n_rad)), device_id_type=MESH
        )

    opsum[...] = jnp.sum(opacity[...], axis=0)
    for copy in load_x2:
        copy.wait()

    nxt = lax.rem(tile + 1, n_tile)
    prv = lax.rem(tile + n_tile - 1, n_tile)
    has_next = jnp.logical_and(tile != quarter - 1, tile != 3 * quarter - 1)
    has_prev = jnp.logical_and(tile != quarter, tile != 3 * quarter)
    has_above = rad != n_rad - 1
    has_below = rad != 0

    for f in range(F):
        for j in range(3):
            for h in range(halves):
                side = pl.ds(h * LANES, LANES)
                psend[f, 0, j, :, side] = x2[h, pl.ds(f * L * R + R - 3 + j, L, stride=R), :]
                psend[f, 1, j, :, side] = x2[h, pl.ds(f * L * R + j, L, stride=R), :]

    pl.semaphore_wait(barrier, n_tile - 1 + n_rad - 1)

    lvl_up = pltpu.make_async_remote_copy(
        src_ref=f4.at[:, pl.ds(L - 3, 3)], dst_ref=ext.at[:, pl.ds(0, 3)],
        send_sem=lvl_send.at[0], recv_sem=lvl_recv.at[0],
        device_id=(tile, lax.rem(rad + 1, n_rad)), device_id_type=MESH,
    )
    lvl_down = pltpu.make_async_remote_copy(
        src_ref=f4.at[:, pl.ds(0, 3)], dst_ref=ext.at[:, pl.ds(L + 3, 3)],
        send_sem=lvl_send.at[1], recv_sem=lvl_recv.at[1],
        device_id=(tile, lax.rem(rad + n_rad - 1, n_rad)), device_id_type=MESH,
    )

    @pl.when(has_above)
    def _():
        lvl_up.start()

    @pl.when(has_below)
    def _():
        lvl_down.start()

    op_copies = []
    for d in range(1, n_rad):
        copy = pltpu.make_async_remote_copy(
            src_ref=opsum, dst_ref=oprecv.at[d - 1],
            send_sem=op_send.at[d - 1], recv_sem=op_recv.at[d - 1],
            device_id=(tile, lax.rem(rad + d, n_rad)), device_id_type=MESH,
        )
        copy.start()
        op_copies.append(copy)

    half = F // 2
    relays = inner < n_tile
    place = lax.rem(tile, inner)
    crosses = (place == inner - 1, place == 0)
    partner = (nxt, prv)
    via = (tile - (inner - 1), tile + (inner - 1))
    sends = (has_next, has_prev)
    origin = (lax.rem(tile + inner - 1, n_tile), lax.rem(tile + n_tile - inner + 1, n_tile))
    forwards = (
        jnp.logical_and(
            crosses[1],
            jnp.logical_and(origin[0] != quarter - 1, origin[0] != 3 * quarter - 1),
        ),
        jnp.logical_and(
            crosses[0], jnp.logical_and(origin[1] != quarter, origin[1] != 3 * quarter)
        ),
    )
    goal = (lax.rem(origin[0] + 1, n_tile), lax.rem(origin[1] + n_tile - 1, n_tile))

    def row_copy(f, way):
        return pltpu.make_async_remote_copy(
            src_ref=psend.at[f, way], dst_ref=precv.at[f, way],
            send_sem=row_send.at[f, way], recv_sem=row_recv.at[f, way],
            device_id=(partner[way], rad), device_id_type=MESH,
        )

    def hop_copy(f, way):
        return pltpu.make_async_remote_copy(
            src_ref=psend.at[f, way], dst_ref=relay.at[f - half, way],
            send_sem=row_send.at[f, way], recv_sem=hop_recv.at[f - half, way],
            device_id=(via[way], rad), device_id_type=MESH,
        )

    def forward_copy(f, way):
        return pltpu.make_async_remote_copy(
            src_ref=relay.at[f - half, way], dst_ref=precv.at[f, way],
            send_sem=fwd_send.at[f - half, way], recv_sem=row_recv.at[f, way],
            device_id=(goal[way], rad), device_id_type=MESH,
        )

    def hops(f):
        return relays and f >= half

    def start_rows(fields, hopping):
        for f in fields:
            for way in range(2):
                if not hops(f):
                    if not hopping:
                        @pl.when(sends[way])
                        def _():
                            row_copy(f, way).start()
                elif hopping:
                    @pl.when(jnp.logical_and(sends[way], crosses[way]))
                    def _():
                        hop_copy(f, way).start()
                else:
                    @pl.when(jnp.logical_and(sends[way], jnp.logical_not(crosses[way])))
                    def _():
                        row_copy(f, way).start()

    start_rows(range(half, F), True)
    start_rows(range(EARLY), False)

    values = jnp.zeros((V, T), jnp.float32)
    diff = lax.broadcasted_iota(jnp.int32, (C, T), 0) - dcol[...]
    rows = drow[...]
    for r in range(R):
        weights = []
        for b in range(4):
            w = jnp.zeros((1, T), jnp.float32)
            for a in range(4):
                w = jnp.where(rows + a == r, lagrange[4 * a + b : 4 * a + b + 1, :], w)
            weights.append(w)
        g = jnp.where(diff == 0, weights[0], 0.0)
        for b in range(1, 4):
            g = jnp.where(diff == b, weights[b], g)
        gh, gl = split(g)
        xh, xl = split(
            jnp.concatenate([x2[h, pl.ds(r, V, stride=R), :] for h in range(halves)], axis=1)
        )
        values = values + (dot(xh, gh) + (dot(xl, gh) + dot(xh, gl)))

    target = ttile[...]
    kinds = max(16, n_tile)
    hot = (lax.broadcasted_iota(jnp.int32, (kinds, T), 0) == target).astype(jnp.float32)
    before = (
        lax.broadcasted_iota(jnp.int32, (T, T), 0) < lax.broadcasted_iota(jnp.int32, (T, T), 1)
    ).astype(jnp.float32)
    earlier = dot(hot.astype(jnp.bfloat16), before.astype(jnp.bfloat16))
    rank = jnp.sum(earlier * hot, axis=0, keepdims=True)
    key = target * cap + rank.astype(jnp.int32)
    lane_slot = lax.rem(lax.broadcasted_iota(jnp.int32, (LANES, T), 0), cap)
    vh, vl = split(values)
    label = tcell[...]
    side = lax.broadcasted_iota(jnp.int32, (16, T), 0)
    label = jnp.where(
        side == 0, label // C + 1, jnp.where(side == 1, lax.rem(label, C), 0)
    ).astype(jnp.float32).astype(jnp.bfloat16)
    stacked = jnp.concatenate([vh, vl, label], axis=0)
    lane_group = lax.broadcasted_iota(jnp.int32, (VP, LANES), 1) // cap

    def chunk(d):
        first = lax.rem(tile + d, n_tile) * cap
        chosen = (key == lane_slot + first).astype(jnp.float32).astype(jnp.bfloat16)
        moved = lax.dot_general(stacked, chosen, NT, preferred_element_type=jnp.float32)
        full = moved[:V] + moved[V : 2 * V]
        picked = full[:VP]
        for g in range(1, pack):
            picked = jnp.where(lane_group == g, full[g * VP : (g + 1) * VP], picked)
        return picked, moved[2 * V : 2 * V + 8]

    picked, marks = chunk(0)
    inc[0, pl.ds(0, VP)] = picked
    inc[0, pl.ds(VP, 8)] = marks

    def a2a_copy(d):
        return pltpu.make_async_remote_copy(
            src_ref=chunks.at[d], dst_ref=inc.at[d],
            send_sem=a2a_send.at[d], recv_sem=a2a_recv.at[d],
            device_id=(lax.rem(tile + d, n_tile), rad), device_id_type=MESH,
        )

    def send_chunk(d):
        picked, marks = chunk(d)
        chunks[d, pl.ds(0, VP)] = picked
        chunks[d, pl.ds(VP, 8)] = marks
        a2a_copy(d).start()

    if n_tile <= 8:
        for d in range(1, n_tile):
            send_chunk(d)
    else:
        lax.fori_loop(1, n_tile, lambda d, c: (send_chunk(d), c)[1], 0)

    start_rows(range(EARLY, F), False)
    if relays:
        for f in range(half, F):
            for way in range(2):
                @pl.when(forwards[way])
                def _():
                    hop_copy(f, way).wait_recv()
                    forward_copy(f, way).start()

    load_ext.wait()
    zeros3 = jnp.zeros((F, 3, R, C), jnp.float32)

    @pl.when(has_below)
    def _():
        lvl_up.wait_recv()

    @pl.when(jnp.logical_not(has_below))
    def _():
        ext[:, pl.ds(0, 3)] = zeros3

    @pl.when(has_above)
    def _():
        lvl_down.wait_recv()

    @pl.when(jnp.logical_not(has_above))
    def _():
        ext[:, pl.ds(L + 3, 3)] = zeros3

    column = lax.broadcasted_iota(jnp.int32, (STEP, R, C), 2)

    def local_part(i, carry):
        f = i // (L // STEP)
        l = lax.rem(i, L // STEP) * STEP
        u = ext[f, pl.ds(l + 3, STEP)]
        speed1 = ext[1, pl.ds(l + 3, STEP)]
        speed3 = ext[3, pl.ds(l + 3, STEP)]
        ups = [ext[f, pl.ds(l + 3 + k, STEP)] for k in (1, 2, 3)]
        downs = [ext[f, pl.ds(l + 3 - k, STEP)] for k in (1, 2, 3)]
        first, second = pair_terms(u, ups, downs)
        total = VISCOSITY * second - speed1 * first
        ups = [jnp.where(column < C - k, pltpu.roll(u, C - k, 2), 0.0) for k in (1, 2, 3)]
        downs = [jnp.where(column >= k, pltpu.roll(u, k, 2), 0.0) for k in (1, 2, 3)]
        first, second = pair_terms(u, ups, downs)
        acc[f, pl.ds(l, STEP)] = total + (VISCOSITY * second - speed3 * first)
        return carry

    lax.fori_loop(0, F * (L // STEP), local_part, 0)

    above = jnp.zeros((R, C), jnp.float32)
    for d in range(1, n_rad):
        op_copies[d - 1].wait_recv()
        above = above + jnp.where(rad >= d, oprecv[d - 1], 0.0)

    def cool(l, so_far):
        mine = opacity[l]
        depth = so_far + 0.5 * mine
        acc[7, l] = acc[7, l] - COOL_RATE * jnp.exp(-depth) * ext[7, l + 3]
        return so_far + mine

    lax.fori_loop(0, L, cool, above)

    for d in range(1, n_tile):
        a2a_copy(d).wait_recv()
    group_of = lax.broadcasted_iota(jnp.int32, (1, LANES), 1) // cap
    row_marks = []
    column_marks = []
    for d0 in range(0, n_tile, pack):
        lanes = pl.ds(d0 // pack * LANES, LANES)
        parts = [inc[d0 + j] for j in range(pack)]
        for g in range(pack):
            joined = None
            for j in range(pack):
                part = parts[j][:VP]
                turn = ((j - g) * cap) % LANES
                if turn:
                    part = pltpu.roll(part, turn, 1)
                joined = part if joined is None else jnp.where(lane_group == j, part, joined)
            high, low = split(joined)
            xall[pl.ds(g * VP, VP), lanes] = high
            xall[pl.ds(V + g * VP, VP), lanes] = low
        xall[pl.ds(2 * V, 16), lanes] = jnp.ones((16, LANES), jnp.bfloat16)
        row_mark = parts[0][VP : VP + 1]
        column_mark = parts[0][VP + 1 : VP + 2]
        for j in range(1, pack):
            row_mark = jnp.where(group_of == j, parts[j][VP : VP + 1], row_mark)
            column_mark = jnp.where(group_of == j, parts[j][VP + 1 : VP + 2], column_mark)
        row_marks.append(row_mark)
        column_marks.append(column_mark)
    row_mark = jnp.concatenate(row_marks, axis=1).astype(jnp.int32)
    column_mark = jnp.concatenate(column_marks, axis=1).astype(jnp.int32)
    slots = n_tile * cap
    cell_column = lax.broadcasted_iota(jnp.int32, (C, slots), 0)
    everything = xall[...]
    for r in range(R):
        wanted = jnp.where(row_mark == r + 1, column_mark, -1)
        place = (cell_column == wanted).astype(jnp.float32).astype(jnp.bfloat16)
        got = lax.dot_general(everything, place, NT, preferred_element_type=jnp.float32)
        total = got[:V] + got[V : 2 * V]
        for h in range(halves):
            ghost[h, pl.ds(r, V, stride=R), :] = total[:, h * LANES : (h + 1) * LANES]
        hits[pl.ds(r, 1), :] = got[2 * V : 2 * V + 1]

    row = lax.broadcasted_iota(jnp.int32, (STEP, R, C), 1)
    planes = x2

    def out_copy(f):
        return pltpu.make_async_copy(acc.at[f], out.at[f], out_sem.at[f])

    for f in range(F):
        @pl.when(has_prev)
        def _():
            row_copy(f, 0).wait_recv()

        @pl.when(jnp.logical_not(has_prev))
        def _():
            precv[f, 0] = jnp.zeros((3, L, C), jnp.float32)

        @pl.when(has_next)
        def _():
            row_copy(f, 1).wait_recv()

        @pl.when(jnp.logical_not(has_next))
        def _():
            precv[f, 1] = jnp.zeros((3, L, C), jnp.float32)

        for j in range(3):
            for h in range(halves):
                side = pl.ds(h * LANES, LANES)
                planes[h, pl.ds(f * L * R + R - 3 + j, L, stride=R), :] = precv[f, 0, j, :, side]
                planes[h, pl.ds(f * L * R + j, L, stride=R), :] = precv[f, 1, j, :, side]

        def row_part(i, carry):
            l = i * STEP
            u = ext[f, pl.ds(l + 3, STEP)]
            speed2 = ext[2, pl.ds(l + 3, STEP)]
            at = pl.ds(pl.multiple_of((f * L + l) * R, STEP * R), STEP * R)
            edge = jnp.concatenate(
                [planes[h, at, :].reshape(STEP, R, LANES) for h in range(halves)], axis=2
            )
            arrived = jnp.concatenate(
                [ghost[h, at, :].reshape(STEP, R, LANES) for h in range(halves)], axis=2
            )
            ups = [pltpu.roll(jnp.where(row < k, edge, u), R - k, 1) for k in (1, 2, 3)]
            downs = [pltpu.roll(jnp.where(row >= R - k, edge, u), k, 1) for k in (1, 2, 3)]
            first, second = pair_terms(u, ups, downs)
            total = acc[f, pl.ds(l, STEP)] + (VISCOSITY * second - speed2 * first)
            total = total + COUPLING * (arrived - hits[...] * u)
            acc[f, pl.ds(l, STEP)] = u + TIME_STEP * total
            return carry

        lax.fori_loop(0, L // STEP, row_part, 0)
        out_copy(f).start()

    @pl.when(has_above)
    def _():
        lvl_up.wait_send()

    @pl.when(has_below)
    def _():
        lvl_down.wait_send()

    for copy in op_copies:
        copy.wait_send()
    for d in range(1, n_tile):
        a2a_copy(d).wait_send()
    for f in range(F):
        for way in range(2):
            @pl.when(sends[way])
            def _():
                row_copy(f, way).wait_send()

            if hops(f):
                @pl.when(forwards[way])
                def _():
                    forward_copy(f, way).wait_send()

    for f in range(F):
        out_copy(f).wait()


def shards(n_tile, n_rad, inner, fields, opacity, donor_row, donor_column, target_tile, target_cell, lagrange):
    F, L, R, C = fields.shape
    V = F * L
    T = donor_row.shape[0]
    cap = max(16, 2 * T // n_tile)
    pack = LANES // cap
    VP = V // pack
    hbm = pl.BlockSpec(memory_space=pl.ANY)
    vmem = pl.BlockSpec(memory_space=pltpu.VMEM)
    dma = pltpu.SemaphoreType.DMA
    f32 = jnp.float32
    return pl.pallas_call(
        functools.partial(kernel, n_tile, n_rad, inner, cap),
        out_shape=jax.ShapeDtypeStruct(fields.shape, f32),
        in_specs=[hbm, hbm] + [vmem] * 6,
        out_specs=hbm,
        scratch_shapes=[
            pltpu.VMEM((C // LANES, V * R, LANES), f32),
            pltpu.VMEM((F, L + 6, R, C), f32),
            pltpu.VMEM((F, L, R, C), f32),
            pltpu.VMEM((F, 2, 3, L, C), f32),
            pltpu.VMEM((F, 2, 3, L, C), f32),
            pltpu.VMEM((F - F // 2, 2, 3, L, C), f32),
            pltpu.VMEM((C // LANES, V * R, LANES), f32),
            pltpu.VMEM((R, C), f32),
            pltpu.VMEM((n_tile, VP + 8, LANES), f32),
            pltpu.VMEM((n_tile, VP + 8, LANES), f32),
            pltpu.VMEM((2 * V + 16, n_tile * cap), jnp.bfloat16),
            pltpu.VMEM((R, C), f32),
            pltpu.VMEM((n_rad - 1, R, C), f32),
            dma((C // LANES,)),
            dma(()),
            dma((2,)),
            dma((2,)),
            dma((F, 2)),
            dma((F, 2)),
            dma((F - F // 2, 2)),
            dma((F - F // 2, 2)),
            dma((n_rad - 1,)),
            dma((n_rad - 1,)),
            dma((n_tile,)),
            dma((n_tile,)),
            dma((F,)),
        ],
        compiler_params=pltpu.CompilerParams(collective_id=0, has_side_effects=True),
    )(
        fields,
        fields.reshape(V * R, C),
        opacity,
        donor_row.reshape(1, T),
        donor_column.reshape(1, T),
        target_tile.reshape(1, T),
        target_cell.reshape(1, T),
        lagrange,
    )


def line_length(mesh):
    devices = mesh.devices[:, 0]
    spots = [getattr(device, "coords", None) for device in devices]
    if spots[0] is None:
        return len(spots)
    moved = [k for k in range(3) if len(spots) > 1 and spots[1][k] != spots[0][k]]
    if len(moved) != 1:
        return len(spots)
    count = 1
    while count < len(spots) and all(
        spots[count][k] == spots[0][k] for k in range(3) if k != moved[0]
    ):
        count += 1
    return count


def solution(mesh):
    in_specs = (
        P(None, "rad", "tile", None),
        P("rad", "tile", None),
        P("tile"),
        P("tile"),
        P("tile", None),
        P("tile"),
        P(None, "tile"),
    )
    out_specs = P(None, "rad", "tile", None)
    body = functools.partial(shards, mesh.shape["tile"], mesh.shape["rad"], line_length(mesh))
    return jax.shard_map(body, mesh=mesh, in_specs=in_specs, out_specs=out_specs, check_vma=False)
```

profile of v0, /device:TPU:0, one launch (start us, length us, event | category | flops | bytes accessed | tf_op | source)
XLA Modules:
  0.0 35.9 jit_solution(16363481941690790273)
XLA Ops:
  0.0 33.3 %shard_map.73 = f32[8,24,8,256]{3,2,1,0:T(8,128)} custom-call(f32[8,24,8,256]{3,2,1,0:T(8,128)} %f4.1, f32[1536,256]{1,0:T(8,128)} %bitcast.5, f32[24,8,256]{2,1,0:T(8,128)} %opacity.1, s32[1,256]{1,0:T(1,128)} %bitcast.6, s32[1,256]{1,0:T(1,128)} %bitcast.7, s32[1,256]{1,0:T(1,128)} %bitcast.8, s32[1,256]{1,0:T(1,128)} %bitcast.9, f32[16,256]{1,0:T(8,128)} %lagrange.1), custom_call_target="tpu_custom_call" | custom-call | tf_op jit(solution)/shard_map/pallas_call | solution.py:452
  33.3 2.7 %copy.9 = f32[8,24,8,256]{3,2,1,0:T(8,128)} copy(f32[8,24,8,256]{3,2,1,0:T(8,128)} %shard_map.73) | data formatting | bytes 3145728
where the time goes:
time: 36.1 us; the launch traced here: 35.9 us
  Pallas kernels  33.3 us (92%)
  local copies, waits for them, and re-layouts  2.65 us (7%)
    pallas_call x1, Pallas kernels, shards(): pl.pallas_call(functools.partial(kernel, n_tile, n_rad, inner, cap), out_...  33.3 us
    unnamed x1, local copies, waits for them, and re-layouts  2.65 us

commit v1 on v0

--- a/solution.py
+++ b/solution.py
@@ -13,9 +13,14 @@
 TIME_STEP = 0.2
 MESH = pl.DeviceIdType.MESH
 LANES = 128
+VMEM_LIMIT = 32 << 20
 STEP = 4
 EARLY = 2
 NT = (((1,), (1,)), ((), ()))
+
+
+def in_hbm(x):
+    return pltpu.with_memory_space_constraint(x, pltpu.HBM)
 
 
 def dot(a, b):
@@ -41,10 +46,10 @@
 def kernel(
     n_tile, n_rad, inner, cap,
     f4, f2, opacity, drow, dcol, ttile, tcell, lagrange,
-    out,
-    x2, ext, acc, psend, precv, relay, ghost, hits, chunks, inc, xall, opsum, oprecv,
+    acc,
+    x2, ext, psend, precv, relay, ghost, hits, chunks, inc, xall, opsum, oprecv,
     x2_sem, in_sem, lvl_send, lvl_recv, row_send, row_recv, hop_recv, fwd_send, op_send, op_recv,
-    a2a_send, a2a_recv, out_sem,
+    a2a_send, a2a_recv,
 ):
     F, L, R, C = acc.shape
     V = F * L
@@ -363,9 +368,6 @@
     row = lax.broadcasted_iota(jnp.int32, (STEP, R, C), 1)
     planes = x2
 
-    def out_copy(f):
-        return pltpu.make_async_copy(acc.at[f], out.at[f], out_sem.at[f])
-
     for f in range(F):
         @pl.when(has_prev)
         def _():
@@ -409,7 +411,6 @@
             return carry
 
         lax.fori_loop(0, L // STEP, row_part, 0)
-        out_copy(f).start()
 
     @pl.when(has_above)
     def _():
@@ -434,9 +435,6 @@
                 def _():
                     forward_copy(f, way).wait_send()
 
-    for f in range(F):
-        out_copy(f).wait()
-
 
 def shards(n_tile, n_rad, inner, fields, opacity, donor_row, donor_column, target_tile, target_cell, lagrange):
     F, L, R, C = fields.shape
@@ -445,19 +443,18 @@
     cap = max(16, 2 * T // n_tile)
     pack = LANES // cap
     VP = V // pack
-    hbm = pl.BlockSpec(memory_space=pl.ANY)
+    hbm = pl.BlockSpec(memory_space=pltpu.HBM)
     vmem = pl.BlockSpec(memory_space=pltpu.VMEM)
     dma = pltpu.SemaphoreType.DMA
     f32 = jnp.float32
     return pl.pallas_call(
         functools.partial(kernel, n_tile, n_rad, inner, cap),
-        out_shape=jax.ShapeDtypeStruct(fields.shape, f32),
+        out_shape=pltpu.VMEM(fields.shape, f32),
         in_specs=[hbm, hbm] + [vmem] * 6,
-        out_specs=hbm,
+        out_specs=vmem,
         scratch_shapes=[
             pltpu.VMEM((C // LANES, V * R, LANES), f32),
             pltpu.VMEM((F, L + 6, R, C), f32),
-            pltpu.VMEM((F, L, R, C), f32),
             pltpu.VMEM((F, 2, 3, L, C), f32),
             pltpu.VMEM((F, 2, 3, L, C), f32),
             pltpu.VMEM((F - F // 2, 2, 3, L, C), f32),
@@ -480,18 +477,19 @@
             dma((n_rad - 1,)),
             dma((n_tile,)),
             dma((n_tile,)),
-            dma((F,)),
         ],
-        compiler_params=pltpu.CompilerParams(collective_id=0, has_side_effects=True),
+        compiler_params=pltpu.CompilerParams(
+            collective_id=0, has_side_effects=True, vmem_limit_bytes=VMEM_LIMIT
+        ),
     )(
-        fields,
-        fields.reshape(V * R, C),
-        opacity,
-        donor_row.reshape(1, T),
-        donor_column.reshape(1, T),
-        target_tile.reshape(1, T),
-        target_cell.reshape(1, T),
-        lagrange,
+        in_hbm(fields),
+        in_hbm(fields.reshape(V * R, C)),
+        in_hbm(opacity),
+        in_hbm(donor_row.reshape(1, T)),
+        in_hbm(donor_column.reshape(1, T)),
+        in_hbm(target_tile.reshape(1, T)),
+        in_hbm(target_cell.reshape(1, T)),
+        in_hbm(lagrange),
     )
 
 

time: 36.1 us -> 33.9 us (0.939)
  local copies, waits for them, and re-layouts: 2.65 us -> 1.15 us
  Pallas kernels: 33.3 us -> 32.6 us
    unnamed x1, local copies, waits for them, and re-layouts: 2.65 us -> 1.15 us
    pallas_call x1, Pallas kernels: 33.3 us -> 32.6 us  [shards(): pl.pallas_call(functools.partial(kernel, n_tile, n_rad, inner, cap), out_...]
where the time goes in v1:
time: 33.9 us; the launch traced here: 33.7 us
  Pallas kernels  32.6 us (96%)
  local copies, waits for them, and re-layouts  1.15 us (3%)
    pallas_call x1, Pallas kernels, shards(): pl.pallas_call(functools.partial(kernel, n_tile, n_rad, inner, cap), out_...  32.6 us
    unnamed x1, local copies, waits for them, and re-layouts  1.15 us

profile of v1, /device:TPU:0, one launch (start us, length us, event | category | flops | bytes accessed | tf_op | source)
XLA Modules:
  0.0 33.7 jit_solution(15096466505647212966)
XLA Ops:
  0.0 32.6 %shard_map.73 = f32[8,24,8,256]{3,2,1,0:T(8,128)S(1)} custom-call(f32[8,24,8,256]{3,2,1,0:T(8,128)} %f4.1, f32[1536,256]{1,0:T(8,128)} %bitcast.5, f32[24,8,256]{2,1,0:T(8,128)} %opacity.1, s32[1,256]{1,0:T(1,128)} %bitcast.6, s32[1,256]{1,0:T(1,128)} %bitcast.7, s32[1,256]{1,0:T(1,128)} %bitcast.8, s32[1,256]{1,0:T(1,128)} %bitcast.9, f32[16,256]{1,0:T(8,128)} %lagrange.1), custom_call_target="tpu_custom_call" | custom-call | tf_op jit(solution)/shard_map/pallas_call | solution.py:450
  32.6 1.1 %copy.9 = f32[8,24,8,256]{3,2,1,0:T(8,128)} copy(f32[8,24,8,256]{3,2,1,0:T(8,128)S(1)} %shard_map.73) | data formatting | bytes 3145728

commit v2 on v1

--- a/solution.py
+++ b/solution.py
@@ -15,7 +15,9 @@
 LANES = 128
 VMEM_LIMIT = 32 << 20
 STEP = 4
-EARLY = 2
+EARLY = 3
+CROSS = 2
+FIRST = 1
 NT = (((1,), (1,)), ((), ()))
 
 
@@ -45,11 +47,12 @@
 
 def kernel(
     n_tile, n_rad, inner, cap,
-    f4, f2, opacity, drow, dcol, ttile, tcell, lagrange,
+    f4, f2, opacity_in, drow_in, dcol_in, ttile_in, tcell_in, lagrange_in,
     acc,
-    x2, ext, psend, precv, relay, ghost, hits, chunks, inc, xall, opsum, oprecv,
-    x2_sem, in_sem, lvl_send, lvl_recv, row_send, row_recv, hop_recv, fwd_send, op_send, op_recv,
-    a2a_send, a2a_recv,
+    x2, ext, edge, relay, ghost, hits, chunks, inc, xall, opsum, oprecv,
+    opacity, drow, dcol, ttile, tcell, lagrange,
+    x2_sem, in_sem, small_sem, side_sem, rad_sem, far_sem, lvl_send, lvl_recv, row_send, row_recv, hop_recv, fwd_send,
+    op_send, op_recv, a2a_send, a2a_recv,
 ):
     F, L, R, C = acc.shape
     V = F * L
@@ -59,30 +62,65 @@
     tile = lax.axis_index("tile")
     rad = lax.axis_index("rad")
     quarter = n_tile // 4
+    place = lax.rem(tile, inner)
+    line = tile // inner
+
+    def each(count, visit):
+        if count <= 8:
+            for d in range(1, count):
+                visit(d)
+        else:
+            lax.fori_loop(1, count, lambda d, c: (visit(d), c)[1], 0)
+
+    def beside(other):
+        across = jnp.abs(lax.rem(other, inner) - place)
+        return jnp.logical_and(
+            other // inner == line, jnp.logical_or(across == 1, across == inner - 1)
+        )
+
+    def count(flag):
+        return flag.astype(jnp.int32)
+
+    side_higher = count(place < inner - 1)
+    if inner > 2:
+        side_higher = side_higher + count(place == 0)
+
+    def signal(semaphore, to_tile, to_rad):
+        pl.semaphore_signal(semaphore, inc=1, device_id=(to_tile, to_rad), device_id_type=MESH)
+
+    barrier = pltpu.get_barrier_semaphore()
+
+    def announce_tile(d):
+        @pl.when(tile + d < n_tile)
+        def _():
+            signal(barrier, tile + d, rad)
+
+    def announce_rad(d):
+        @pl.when(rad + d < n_rad)
+        def _():
+            signal(barrier, tile, rad + d)
+
+    each(n_tile, announce_tile)
+    each(n_rad, announce_rad)
 
     halves = C // LANES
     load_x2 = [
         pltpu.make_async_copy(f2.at[:, pl.ds(h * LANES, LANES)], x2.at[h], x2_sem.at[h])
         for h in range(halves)
     ]
+    load_small = [
+        pltpu.make_async_copy(source, kept, small_sem.at[k])
+        for k, (source, kept) in enumerate(
+            [
+                (dcol_in, dcol), (drow_in, drow), (lagrange_in, lagrange), (ttile_in, ttile),
+                (tcell_in, tcell), (opacity_in, opacity),
+            ]
+        )
+    ]
     load_ext = pltpu.make_async_copy(f4, ext.at[:, pl.ds(3, L)], in_sem)
-    for copy in load_x2:
+    for copy in load_x2 + load_small:
         copy.start()
     load_ext.start()
-
-    barrier = pltpu.get_barrier_semaphore()
-    for d in range(1, n_tile):
-        pl.semaphore_signal(
-            barrier, inc=1, device_id=(lax.rem(tile + d, n_tile), rad), device_id_type=MESH
-        )
-    for d in range(1, n_rad):
-        pl.semaphore_signal(
-            barrier, inc=1, device_id=(tile, lax.rem(rad + d, n_rad)), device_id_type=MESH
-        )
-
-    opsum[...] = jnp.sum(opacity[...], axis=0)
-    for copy in load_x2:
-        copy.wait()
 
     nxt = lax.rem(tile + 1, n_tile)
     prv = lax.rem(tile + n_tile - 1, n_tile)
@@ -91,47 +129,8 @@
     has_above = rad != n_rad - 1
     has_below = rad != 0
 
-    for f in range(F):
-        for j in range(3):
-            for h in range(halves):
-                side = pl.ds(h * LANES, LANES)
-                psend[f, 0, j, :, side] = x2[h, pl.ds(f * L * R + R - 3 + j, L, stride=R), :]
-                psend[f, 1, j, :, side] = x2[h, pl.ds(f * L * R + j, L, stride=R), :]
-
-    pl.semaphore_wait(barrier, n_tile - 1 + n_rad - 1)
-
-    lvl_up = pltpu.make_async_remote_copy(
-        src_ref=f4.at[:, pl.ds(L - 3, 3)], dst_ref=ext.at[:, pl.ds(0, 3)],
-        send_sem=lvl_send.at[0], recv_sem=lvl_recv.at[0],
-        device_id=(tile, lax.rem(rad + 1, n_rad)), device_id_type=MESH,
-    )
-    lvl_down = pltpu.make_async_remote_copy(
-        src_ref=f4.at[:, pl.ds(0, 3)], dst_ref=ext.at[:, pl.ds(L + 3, 3)],
-        send_sem=lvl_send.at[1], recv_sem=lvl_recv.at[1],
-        device_id=(tile, lax.rem(rad + n_rad - 1, n_rad)), device_id_type=MESH,
-    )
-
-    @pl.when(has_above)
-    def _():
-        lvl_up.start()
-
-    @pl.when(has_below)
-    def _():
-        lvl_down.start()
-
-    op_copies = []
-    for d in range(1, n_rad):
-        copy = pltpu.make_async_remote_copy(
-            src_ref=opsum, dst_ref=oprecv.at[d - 1],
-            send_sem=op_send.at[d - 1], recv_sem=op_recv.at[d - 1],
-            device_id=(tile, lax.rem(rad + d, n_rad)), device_id_type=MESH,
-        )
-        copy.start()
-        op_copies.append(copy)
-
     half = F // 2
     relays = inner < n_tile
-    place = lax.rem(tile, inner)
     crosses = (place == inner - 1, place == 0)
     partner = (nxt, prv)
     via = (tile - (inner - 1), tile + (inner - 1))
@@ -147,24 +146,25 @@
         ),
     )
     goal = (lax.rem(origin[0] + 1, n_tile), lax.rem(origin[1] + n_tile - 1, n_tile))
+    strip = (pl.ds(R - 3, 3), pl.ds(0, 3))
 
     def row_copy(f, way):
         return pltpu.make_async_remote_copy(
-            src_ref=psend.at[f, way], dst_ref=precv.at[f, way],
+            src_ref=f4.at[f, :, strip[way]], dst_ref=edge.at[f, :, strip[way]],
             send_sem=row_send.at[f, way], recv_sem=row_recv.at[f, way],
             device_id=(partner[way], rad), device_id_type=MESH,
         )
 
     def hop_copy(f, way):
         return pltpu.make_async_remote_copy(
-            src_ref=psend.at[f, way], dst_ref=relay.at[f - half, way],
+            src_ref=f4.at[f, :, strip[way]], dst_ref=relay.at[f - half, :, strip[way]],
             send_sem=row_send.at[f, way], recv_sem=hop_recv.at[f - half, way],
             device_id=(via[way], rad), device_id_type=MESH,
         )
 
     def forward_copy(f, way):
         return pltpu.make_async_remote_copy(
-            src_ref=relay.at[f - half, way], dst_ref=precv.at[f, way],
+            src_ref=relay.at[f - half, :, strip[way]], dst_ref=edge.at[f, :, strip[way]],
             send_sem=fwd_send.at[f - half, way], recv_sem=row_recv.at[f, way],
             device_id=(goal[way], rad), device_id_type=MESH,
         )
@@ -172,25 +172,104 @@
     def hops(f):
         return relays and f >= half
 
-    def start_rows(fields, hopping):
+    def start_hops(way):
+        for f in range(half, F):
+            if hops(f):
+                @pl.when(jnp.logical_and(sends[way], crosses[way]))
+                def _():
+                    hop_copy(f, way).start()
+
+    def start_beside(way, fields):
+        for f in fields:
+            @pl.when(jnp.logical_and(sends[way], jnp.logical_not(crosses[way])))
+            def _():
+                row_copy(f, way).start()
+
+    def start_crossing(fields, lower):
         for f in fields:
             for way in range(2):
                 if not hops(f):
-                    if not hopping:
-                        @pl.when(sends[way])
-                        def _():
-                            row_copy(f, way).start()
-                elif hopping:
-                    @pl.when(jnp.logical_and(sends[way], crosses[way]))
-                    def _():
-                        hop_copy(f, way).start()
-                else:
-                    @pl.when(jnp.logical_and(sends[way], jnp.logical_not(crosses[way])))
+                    ready = partner[way] < tile if lower else partner[way] > tile
+
+                    @pl.when(jnp.logical_and(jnp.logical_and(sends[way], crosses[way]), ready))
                     def _():
                         row_copy(f, way).start()
 
-    start_rows(range(half, F), True)
-    start_rows(range(EARLY), False)
+    def forward(f):
+        for way in range(2):
+            @pl.when(forwards[way])
+            def _():
+                hop_copy(f, way).wait_recv()
+                forward_copy(f, way).start()
+
+    lvl_up = pltpu.make_async_remote_copy(
+        src_ref=f4.at[:, pl.ds(L - 3, 3)], dst_ref=ext.at[:, pl.ds(0, 3)],
+        send_sem=lvl_send.at[0], recv_sem=lvl_recv.at[0],
+        device_id=(tile, lax.rem(rad + 1, n_rad)), device_id_type=MESH,
+    )
+    lvl_down = pltpu.make_async_remote_copy(
+        src_ref=f4.at[:, pl.ds(0, 3)], dst_ref=ext.at[:, pl.ds(L + 3, 3)],
+        send_sem=lvl_send.at[1], recv_sem=lvl_recv.at[1],
+        device_id=(tile, lax.rem(rad + n_rad - 1, n_rad)), device_id_type=MESH,
+    )
+    op_copies = [
+        pltpu.make_async_remote_copy(
+            src_ref=opsum, dst_ref=oprecv.at[d - 1],
+            send_sem=op_send.at[d - 1], recv_sem=op_recv.at[d - 1],
+            device_id=(tile, lax.rem(rad + d, n_rad)), device_id_type=MESH,
+        )
+        for d in range(1, n_rad)
+    ]
+
+    def await_signals(semaphore, amount):
+        @pl.when(amount > 0)
+        def _():
+            pl.semaphore_wait(semaphore, amount)
+
+    await_signals(barrier, tile + rad)
+
+    def report_tile(d):
+        @pl.when(tile >= d)
+        def _():
+            other = tile - d
+
+            @pl.when(beside(other))
+            def _():
+                signal(side_sem, other, rad)
+
+            @pl.when(jnp.logical_not(beside(other)))
+            def _():
+                signal(far_sem, other, rad)
+
+    def report_rad(d):
+        @pl.when(rad >= d)
+        def _():
+            signal(rad_sem, tile, rad - d)
+
+    each(n_tile, report_tile)
+    each(n_rad, report_rad)
+    start_hops(0)
+    start_beside(1, range(EARLY))
+    start_crossing(range(CROSS), True)
+
+    @pl.when(has_below)
+    def _():
+        lvl_down.start()
+
+    await_signals(side_sem, side_higher)
+    start_hops(1)
+    start_beside(0, range(EARLY))
+    await_signals(rad_sem, n_rad - 1 - rad)
+
+    @pl.when(has_above)
+    def _():
+        lvl_up.start()
+
+    for copy in load_small:
+        copy.wait()
+    opsum[...] = jnp.sum(opacity[...], axis=0)
+    for copy in load_x2:
+        copy.wait()
 
     values = jnp.zeros((V, T), jnp.float32)
     diff = lax.broadcasted_iota(jnp.int32, (C, T), 0) - dcol[...]
@@ -240,37 +319,34 @@
             picked = jnp.where(lane_group == g, full[g * VP : (g + 1) * VP], picked)
         return picked, moved[2 * V : 2 * V + 8]
 
+    await_signals(far_sem, n_tile - 1 - tile - side_higher)
+    start_crossing(range(CROSS), False)
+
     picked, marks = chunk(0)
     inc[0, pl.ds(0, VP)] = picked
     inc[0, pl.ds(VP, 8)] = marks
+    used = pl.ds(0, VP + 2)
 
     def a2a_copy(d):
         return pltpu.make_async_remote_copy(
-            src_ref=chunks.at[d], dst_ref=inc.at[d],
+            src_ref=chunks.at[d, used], dst_ref=inc.at[d, used],
             send_sem=a2a_send.at[d], recv_sem=a2a_recv.at[d],
             device_id=(lax.rem(tile + d, n_tile), rad), device_id_type=MESH,
         )
 
-    def send_chunk(d):
+    def fill_chunk(d):
         picked, marks = chunk(d)
         chunks[d, pl.ds(0, VP)] = picked
         chunks[d, pl.ds(VP, 8)] = marks
-        a2a_copy(d).start()
-
-    if n_tile <= 8:
-        for d in range(1, n_tile):
-            send_chunk(d)
-    else:
-        lax.fori_loop(1, n_tile, lambda d, c: (send_chunk(d), c)[1], 0)
-
-    start_rows(range(EARLY, F), False)
-    if relays:
-        for f in range(half, F):
-            for way in range(2):
-                @pl.when(forwards[way])
-                def _():
-                    hop_copy(f, way).wait_recv()
-                    forward_copy(f, way).start()
+
+    each(n_tile, fill_chunk)
+    each(n_tile, lambda d: a2a_copy(d).start())
+    for copy in op_copies:
+        copy.start()
+    start_crossing(range(CROSS, F), True)
+    start_crossing(range(CROSS, F), False)
+    start_beside(1, range(EARLY, F))
+    start_beside(0, range(EARLY, F))
 
     load_ext.wait()
     zeros3 = jnp.zeros((F, 3, R, C), jnp.float32)
@@ -291,11 +367,20 @@
     def _():
         ext[:, pl.ds(L + 3, 3)] = zeros3
 
+    no_rows = jnp.zeros((F, L, 3, C), jnp.float32)
+
+    @pl.when(jnp.logical_not(has_prev))
+    def _():
+        edge[:, :, strip[0]] = no_rows
+
+    @pl.when(jnp.logical_not(has_next))
+    def _():
+        edge[:, :, strip[1]] = no_rows
+
     column = lax.broadcasted_iota(jnp.int32, (STEP, R, C), 2)
 
-    def local_part(i, carry):
-        f = i // (L // STEP)
-        l = lax.rem(i, L // STEP) * STEP
+    def local_part(f, i, carry):
+        l = i * STEP
         u = ext[f, pl.ds(l + 3, STEP)]
         speed1 = ext[1, pl.ds(l + 3, STEP)]
         speed3 = ext[3, pl.ds(l + 3, STEP)]
@@ -309,7 +394,10 @@
         acc[f, pl.ds(l, STEP)] = total + (VISCOSITY * second - speed3 * first)
         return carry
 
-    lax.fori_loop(0, F * (L // STEP), local_part, 0)
+    for f in range(F):
+        lax.fori_loop(0, L // STEP, functools.partial(local_part, f), 0)
+        if relays and FIRST <= f < FIRST + F - half:
+            forward(half + f - FIRST)
 
     above = jnp.zeros((R, C), jnp.float32)
     for d in range(1, n_rad):
@@ -366,44 +454,27 @@
         hits[pl.ds(r, 1), :] = got[2 * V : 2 * V + 1]
 
     row = lax.broadcasted_iota(jnp.int32, (STEP, R, C), 1)
-    planes = x2
 
     for f in range(F):
         @pl.when(has_prev)
         def _():
             row_copy(f, 0).wait_recv()
 
-        @pl.when(jnp.logical_not(has_prev))
-        def _():
-            precv[f, 0] = jnp.zeros((3, L, C), jnp.float32)
-
         @pl.when(has_next)
         def _():
             row_copy(f, 1).wait_recv()
-
-        @pl.when(jnp.logical_not(has_next))
-        def _():
-            precv[f, 1] = jnp.zeros((3, L, C), jnp.float32)
-
-        for j in range(3):
-            for h in range(halves):
-                side = pl.ds(h * LANES, LANES)
-                planes[h, pl.ds(f * L * R + R - 3 + j, L, stride=R), :] = precv[f, 0, j, :, side]
-                planes[h, pl.ds(f * L * R + j, L, stride=R), :] = precv[f, 1, j, :, side]
 
         def row_part(i, carry):
             l = i * STEP
             u = ext[f, pl.ds(l + 3, STEP)]
             speed2 = ext[2, pl.ds(l + 3, STEP)]
             at = pl.ds(pl.multiple_of((f * L + l) * R, STEP * R), STEP * R)
-            edge = jnp.concatenate(
-                [planes[h, at, :].reshape(STEP, R, LANES) for h in range(halves)], axis=2
-            )
+            rim = edge[f, pl.ds(l, STEP)]
             arrived = jnp.concatenate(
                 [ghost[h, at, :].reshape(STEP, R, LANES) for h in range(halves)], axis=2
             )
-            ups = [pltpu.roll(jnp.where(row < k, edge, u), R - k, 1) for k in (1, 2, 3)]
-            downs = [pltpu.roll(jnp.where(row >= R - k, edge, u), k, 1) for k in (1, 2, 3)]
+            ups = [pltpu.roll(jnp.where(row < k, rim, u), R - k, 1) for k in (1, 2, 3)]
+            downs = [pltpu.roll(jnp.where(row >= R - k, rim, u), k, 1) for k in (1, 2, 3)]
             first, second = pair_terms(u, ups, downs)
             total = acc[f, pl.ds(l, STEP)] + (VISCOSITY * second - speed2 * first)
             total = total + COUPLING * (arrived - hits[...] * u)
@@ -450,14 +521,13 @@
     return pl.pallas_call(
         functools.partial(kernel, n_tile, n_rad, inner, cap),
         out_shape=pltpu.VMEM(fields.shape, f32),
-        in_specs=[hbm, hbm] + [vmem] * 6,
+        in_specs=[hbm] * 8,
         out_specs=vmem,
         scratch_shapes=[
             pltpu.VMEM((C // LANES, V * R, LANES), f32),
             pltpu.VMEM((F, L + 6, R, C), f32),
-            pltpu.VMEM((F, 2, 3, L, C), f32),
-            pltpu.VMEM((F, 2, 3, L, C), f32),
-            pltpu.VMEM((F - F // 2, 2, 3, L, C), f32),
+            pltpu.VMEM((F, L, R, C), f32),
+            pltpu.VMEM((F - F // 2, L, R, C), f32),
             pltpu.VMEM((C // LANES, V * R, LANES), f32),
             pltpu.VMEM((R, C), f32),
             pltpu.VMEM((n_tile, VP + 8, LANES), f32),
@@ -465,8 +535,18 @@
             pltpu.VMEM((2 * V + 16, n_tile * cap), jnp.bfloat16),
             pltpu.VMEM((R, C), f32),
             pltpu.VMEM((n_rad - 1, R, C), f32),
+            pltpu.VMEM((L, R, C), f32),
+            pltpu.VMEM((1, T), jnp.int32),
+            pltpu.VMEM((1, T), jnp.int32),
+            pltpu.VMEM((1, T), jnp.int32),
+            pltpu.VMEM((1, T), jnp.int32),
+            pltpu.VMEM(lagrange.shape, f32),
             dma((C // LANES,)),
             dma(()),
+            dma((6,)),
+            pltpu.SemaphoreType.REGULAR,
+            pltpu.SemaphoreType.REGULAR,
+            pltpu.SemaphoreType.REGULAR,
             dma((2,)),
             dma((2,)),
             dma((F, 2)),

time: 33.9 us -> 31.2 us (0.920)
  the two profiles are of different devices: /device:TPU:0 before, /device:TPU:16 now
where the time goes in v2:
time: 31.2 us; the launch traced here: 31.1 us
  Pallas kernels  29.9 us (96%)
  local copies, waits for them, and re-layouts  1.15 us (4%)
    pallas_call x1, Pallas kernels, shards(): pl.pallas_call(functools.partial(kernel, n_tile, n_rad, inner, cap), out_...  29.9 us
    unnamed x1, local copies, waits for them, and re-layouts  1.15 us

profile of v2, /device:TPU:16, one launch (start us, length us, event | category | flops | bytes accessed | tf_op | source)
XLA Modules:
  0.0 31.1 jit_solution(6575583354369322501)
XLA Ops:
  0.0 29.9 %shard_map.73 = f32[8,24,8,256]{3,2,1,0:T(8,128)S(1)} custom-call(f32[8,24,8,256]{3,2,1,0:T(8,128)} %f4.1, f32[1536,256]{1,0:T(8,128)} %bitcast.5, f32[24,8,256]{2,1,0:T(8,128)} %opacity_in.1, s32[1,256]{1,0:T(1,128)} %bitcast.6, s32[1,256]{1,0:T(1,128)} %bitcast.7, s32[1,256]{1,0:T(1,128)} %bitcast.8, s32[1,256]{1,0:T(1,128)} %bitcast.9, f32[16,256]{1,0:T(8,128)} %lagrange_in.1), custom_call_target="tpu_custom_call" | custom-call | tf_op jit(solution)/shard_map/pallas_call | solution.py:521
  29.9 1.1 %copy.9 = f32[8,24,8,256]{3,2,1,0:T(8,128)} copy(f32[8,24,8,256]{3,2,1,0:T(8,128)S(1)} %shard_map.73) | data formatting | bytes 3145728

commit v3 on v2

--- a/solution.py
+++ b/solution.py
@@ -17,6 +17,10 @@
 STEP = 4
 EARLY = 3
 CROSS = 2
+MORE = 2
+FEWER = 2
+SOON = 2
+ORDER = (0, 1, 4, 5, 6, 2, 3, 7)
 FIRST = 1
 NT = (((1,), (1,)), ((), ()))
 
@@ -51,7 +55,7 @@
     acc,
     x2, ext, edge, relay, ghost, hits, chunks, inc, xall, opsum, oprecv,
     opacity, drow, dcol, ttile, tcell, lagrange,
-    x2_sem, in_sem, small_sem, side_sem, rad_sem, far_sem, lvl_send, lvl_recv, row_send, row_recv, hop_recv, fwd_send,
+    x2_sem, in_sem, small_sem, side_sem, turn_sem, rad_sem, far_sem, lvl_send, lvl_recv, row_send, row_recv, hop_recv, fwd_send,
     op_send, op_recv, a2a_send, a2a_recv,
 ):
     F, L, R, C = acc.shape
@@ -82,6 +86,7 @@
         return flag.astype(jnp.int32)
 
     side_higher = count(place < inner - 1)
+    turn_higher = count(jnp.logical_and(place == inner - 1, tile < n_tile - 1))
     if inner > 2:
         side_higher = side_higher + count(place == 0)
 
@@ -131,6 +136,8 @@
 
     half = F // 2
     relays = inner < n_tile
+    order = [f for f in ORDER if f < F] if F == len(ORDER) else list(range(F))
+    whole = [f for f in order if f < half or f == F - 1 or not relays]
     crosses = (place == inner - 1, place == 0)
     partner = (nxt, prv)
     via = (tile - (inner - 1), tile + (inner - 1))
@@ -157,27 +164,35 @@
 
     def hop_copy(f, way):
         return pltpu.make_async_remote_copy(
-            src_ref=f4.at[f, :, strip[way]], dst_ref=relay.at[f - half, :, strip[way]],
-            send_sem=row_send.at[f, way], recv_sem=hop_recv.at[f - half, way],
+            src_ref=f4.at[f, :, strip[way]], dst_ref=relay.at[f - shared, :, strip[way]],
+            send_sem=row_send.at[f, way], recv_sem=hop_recv.at[f - shared, way],
             device_id=(via[way], rad), device_id_type=MESH,
         )
 
     def forward_copy(f, way):
         return pltpu.make_async_remote_copy(
-            src_ref=relay.at[f - half, :, strip[way]], dst_ref=edge.at[f, :, strip[way]],
-            send_sem=fwd_send.at[f - half, way], recv_sem=row_recv.at[f, way],
+            src_ref=relay.at[f - shared, :, strip[way]], dst_ref=edge.at[f, :, strip[way]],
+            send_sem=fwd_send.at[f - shared, way], recv_sem=row_recv.at[f, way],
             device_id=(goal[way], rad), device_id_type=MESH,
         )
 
-    def hops(f):
-        return relays and f >= half
+    shared = half - 1
+    relayed = [*range(half, F), shared] if relays else []
+    def by_relay(f, way, source):
+        wraps = source == n_tile - 1
+        if f == shared and way == 0 and relays:
+            return jnp.logical_and(wraps, lax.rem(rad, MORE) == 0)
+        if f == F - 1 and way == 0 and relays:
+            return jnp.logical_or(wraps, lax.rem(rad, FEWER) != 0)
+        return jnp.logical_and(tile >= 0, f in relayed and f != shared)
 
     def start_hops(way):
-        for f in range(half, F):
-            if hops(f):
-                @pl.when(jnp.logical_and(sends[way], crosses[way]))
-                def _():
-                    hop_copy(f, way).start()
+        for f in relayed:
+            through = by_relay(f, way, tile)
+
+            @pl.when(jnp.logical_and(jnp.logical_and(sends[way], crosses[way]), through))
+            def _():
+                hop_copy(f, way).start()
 
     def start_beside(way, fields):
         for f in fields:
@@ -185,19 +200,17 @@
             def _():
                 row_copy(f, way).start()
 
-    def start_crossing(fields, lower):
+    def start_crossing(fields, way, ready):
         for f in fields:
-            for way in range(2):
-                if not hops(f):
-                    ready = partner[way] < tile if lower else partner[way] > tile
-
-                    @pl.when(jnp.logical_and(jnp.logical_and(sends[way], crosses[way]), ready))
-                    def _():
-                        row_copy(f, way).start()
+            direct = jnp.logical_and(ready, jnp.logical_not(by_relay(f, way, tile)))
+
+            @pl.when(jnp.logical_and(jnp.logical_and(sends[way], crosses[way]), direct))
+            def _():
+                row_copy(f, way).start()
 
     def forward(f):
         for way in range(2):
-            @pl.when(forwards[way])
+            @pl.when(jnp.logical_and(forwards[way], by_relay(f, way, origin[way])))
             def _():
                 hop_copy(f, way).wait_recv()
                 forward_copy(f, way).start()
@@ -233,11 +246,17 @@
         def _():
             other = tile - d
 
+            after = jnp.logical_and(place == 0, d == 1)
+
             @pl.when(beside(other))
             def _():
                 signal(side_sem, other, rad)
 
-            @pl.when(jnp.logical_not(beside(other)))
+            @pl.when(after)
+            def _():
+                signal(turn_sem, other, rad)
+
+            @pl.when(jnp.logical_not(jnp.logical_or(beside(other), after)))
             def _():
                 signal(far_sem, other, rad)
 
@@ -249,8 +268,9 @@
     each(n_tile, report_tile)
     each(n_rad, report_rad)
     start_hops(0)
-    start_beside(1, range(EARLY))
-    start_crossing(range(CROSS), True)
+    start_beside(1, order[:EARLY])
+    start_crossing(whole[:CROSS], 0, nxt < tile)
+    start_crossing(whole[:CROSS], 1, prv < tile)
 
     @pl.when(has_below)
     def _():
@@ -258,7 +278,9 @@
 
     await_signals(side_sem, side_higher)
     start_hops(1)
-    start_beside(0, range(EARLY))
+    start_beside(0, order[:EARLY])
+    await_signals(turn_sem, turn_higher)
+    start_crossing(whole[:CROSS], 0, nxt > tile)
     await_signals(rad_sem, n_rad - 1 - rad)
 
     @pl.when(has_above)
@@ -319,8 +341,11 @@
             picked = jnp.where(lane_group == g, full[g * VP : (g + 1) * VP], picked)
         return picked, moved[2 * V : 2 * V + 8]
 
-    await_signals(far_sem, n_tile - 1 - tile - side_higher)
-    start_crossing(range(CROSS), False)
+    await_signals(far_sem, n_tile - 1 - tile - side_higher - turn_higher)
+    start_crossing(whole[:CROSS], 1, prv > tile)
+    if relays:
+        for f in relayed[:SOON]:
+            forward(f)
 
     picked, marks = chunk(0)
     inc[0, pl.ds(0, VP)] = picked
@@ -339,14 +364,22 @@
         chunks[d, pl.ds(0, VP)] = picked
         chunks[d, pl.ds(VP, 8)] = marks
 
-    each(n_tile, fill_chunk)
-    each(n_tile, lambda d: a2a_copy(d).start())
+    if n_tile <= 8:
+        turns = sorted(range(1, n_tile), key=lambda d: abs(2 * d - n_tile))
+        for k, d in enumerate(turns):
+            fill_chunk(d)
+            if k:
+                a2a_copy(turns[k - 1]).start()
+        a2a_copy(turns[-1]).start()
+    else:
+        each(n_tile, fill_chunk)
+        each(n_tile, lambda d: a2a_copy(d).start())
     for copy in op_copies:
         copy.start()
-    start_crossing(range(CROSS, F), True)
-    start_crossing(range(CROSS, F), False)
-    start_beside(1, range(EARLY, F))
-    start_beside(0, range(EARLY, F))
+    start_crossing(whole[CROSS:], 0, tile >= 0)
+    start_crossing(whole[CROSS:], 1, tile >= 0)
+    start_beside(1, order[EARLY:])
+    start_beside(0, order[EARLY:])
 
     load_ext.wait()
     zeros3 = jnp.zeros((F, 3, R, C), jnp.float32)
@@ -396,8 +429,9 @@
 
     for f in range(F):
         lax.fori_loop(0, L // STEP, functools.partial(local_part, f), 0)
-        if relays and FIRST <= f < FIRST + F - half:
-            forward(half + f - FIRST)
+        if f >= FIRST:
+            for g in relayed[SOON + f - FIRST : SOON + f - FIRST + 1]:
+                forward(g)
 
     above = jnp.zeros((R, C), jnp.float32)
     for d in range(1, n_rad):
@@ -455,7 +489,7 @@
 
     row = lax.broadcasted_iota(jnp.int32, (STEP, R, C), 1)
 
-    for f in range(F):
+    for f in order:
         @pl.when(has_prev)
         def _():
             row_copy(f, 0).wait_recv()
@@ -501,8 +535,8 @@
             def _():
                 row_copy(f, way).wait_send()
 
-            if hops(f):
-                @pl.when(forwards[way])
+            if f in relayed:
+                @pl.when(jnp.logical_and(forwards[way], by_relay(f, way, origin[way])))
                 def _():
                     forward_copy(f, way).wait_send()
 
@@ -527,7 +561,7 @@
             pltpu.VMEM((C // LANES, V * R, LANES), f32),
             pltpu.VMEM((F, L + 6, R, C), f32),
             pltpu.VMEM((F, L, R, C), f32),
-            pltpu.VMEM((F - F // 2, L, R, C), f32),
+            pltpu.VMEM((F - F // 2 + 1, L, R, C), f32),
             pltpu.VMEM((C // LANES, V * R, LANES), f32),
             pltpu.VMEM((R, C), f32),
             pltpu.VMEM((n_tile, VP + 8, LANES), f32),
@@ -547,12 +581,13 @@
             pltpu.SemaphoreType.REGULAR,
             pltpu.SemaphoreType.REGULAR,
             pltpu.SemaphoreType.REGULAR,
+            pltpu.SemaphoreType.REGULAR,
             dma((2,)),
             dma((2,)),
             dma((F, 2)),
             dma((F, 2)),
-            dma((F - F // 2, 2)),
-            dma((F - F // 2, 2)),
+            dma((F - F // 2 + 1, 2)),
+            dma((F - F // 2 + 1, 2)),
             dma((n_rad - 1,)),
             dma((n_rad - 1,)),
             dma((n_tile,)),

time: 31.2 us -> 30.4 us (0.974)
  the two profiles are of different devices: /device:TPU:16 before, /device:TPU:18 now
where the time goes in v3:
time: 30.4 us; the launch traced here: 30.3 us
  Pallas kernels  29.1 us (96%)
  local copies, waits for them, and re-layouts  1.15 us (4%)
    pallas_call x1, Pallas kernels, shards(): pl.pallas_call(functools.partial(kernel, n_tile, n_rad, inner, cap), out_...  29.1 us
    unnamed x1, local copies, waits for them, and re-layouts  1.15 us

profile of v3, /device:TPU:18, one launch (start us, length us, event | category | flops | bytes accessed | tf_op | source)
XLA Modules:
  0.0 30.3 jit_solution(2968259983422722392)
XLA Ops:
  0.0 29.1 %shard_map.73 = f32[8,24,8,256]{3,2,1,0:T(8,128)S(1)} custom-call(f32[8,24,8,256]{3,2,1,0:T(8,128)} %f4.1, f32[1536,256]{1,0:T(8,128)} %bitcast.5, f32[24,8,256]{2,1,0:T(8,128)} %opacity_in.1, s32[1,256]{1,0:T(1,128)} %bitcast.6, s32[1,256]{1,0:T(1,128)} %bitcast.7, s32[1,256]{1,0:T(1,128)} %bitcast.8, s32[1,256]{1,0:T(1,128)} %bitcast.9, f32[16,256]{1,0:T(8,128)} %lagrange_in.1), custom_call_target="tpu_custom_call" | custom-call | tf_op jit(solution)/shard_map/pallas_call | solution.py:555
  29.1 1.1 %copy.9 = f32[8,24,8,256]{3,2,1,0:T(8,128)} copy(f32[8,24,8,256]{3,2,1,0:T(8,128)S(1)} %shard_map.73) | data formatting | bytes 3145728

commit v4 on v3

--- a/solution.py
+++ b/solution.py
@@ -13,12 +13,21 @@
 TIME_STEP = 0.2
 MESH = pl.DeviceIdType.MESH
 LANES = 128
+EVEN = lambda r: lax.rem(r, 2) == 0
+ODD = lambda r: lax.rem(r, 2) == 1
+ALL = lambda r: r >= 0
+NONE = lambda r: r < 0
+LOW = lambda r: r < 2
+ZERO = lambda r: r == 0
 VMEM_LIMIT = 32 << 20
 STEP = 4
 EARLY = 3
 CROSS = 2
-MORE = 2
-FEWER = 2
+PRE = 3
+HEAD = 0
+CROSS_UP = 2
+MORE = (EVEN, NONE)
+FEWER = (EVEN, NONE)
 SOON = 2
 ORDER = (0, 1, 4, 5, 6, 2, 3, 7)
 FIRST = 1
@@ -53,7 +62,7 @@
     n_tile, n_rad, inner, cap,
     f4, f2, opacity_in, drow_in, dcol_in, ttile_in, tcell_in, lagrange_in,
     acc,
-    x2, ext, edge, relay, ghost, hits, chunks, inc, xall, opsum, oprecv,
+    x2, ext, taps, edge, relay, ghost, hits, chunks, inc, xall, opsum, oprecv,
     opacity, drow, dcol, ttile, tcell, lagrange,
     x2_sem, in_sem, small_sem, side_sem, turn_sem, rad_sem, far_sem, lvl_send, lvl_recv, row_send, row_recv, hop_recv, fwd_send,
     op_send, op_recv, a2a_send, a2a_recv,
@@ -76,38 +85,6 @@
         else:
             lax.fori_loop(1, count, lambda d, c: (visit(d), c)[1], 0)
 
-    def beside(other):
-        across = jnp.abs(lax.rem(other, inner) - place)
-        return jnp.logical_and(
-            other // inner == line, jnp.logical_or(across == 1, across == inner - 1)
-        )
-
-    def count(flag):
-        return flag.astype(jnp.int32)
-
-    side_higher = count(place < inner - 1)
-    turn_higher = count(jnp.logical_and(place == inner - 1, tile < n_tile - 1))
-    if inner > 2:
-        side_higher = side_higher + count(place == 0)
-
-    def signal(semaphore, to_tile, to_rad):
-        pl.semaphore_signal(semaphore, inc=1, device_id=(to_tile, to_rad), device_id_type=MESH)
-
-    barrier = pltpu.get_barrier_semaphore()
-
-    def announce_tile(d):
-        @pl.when(tile + d < n_tile)
-        def _():
-            signal(barrier, tile + d, rad)
-
-    def announce_rad(d):
-        @pl.when(rad + d < n_rad)
-        def _():
-            signal(barrier, tile, rad + d)
-
-    each(n_tile, announce_tile)
-    each(n_rad, announce_rad)
-
     halves = C // LANES
     load_x2 = [
         pltpu.make_async_copy(f2.at[:, pl.ds(h * LANES, LANES)], x2.at[h], x2_sem.at[h])
@@ -123,9 +100,38 @@
         )
     ]
     load_ext = pltpu.make_async_copy(f4, ext.at[:, pl.ds(3, L)], in_sem)
-    for copy in load_x2 + load_small:
-        copy.start()
-    load_ext.start()
+    def beside(other):
+        across = jnp.abs(lax.rem(other, inner) - place)
+        return jnp.logical_and(
+            other // inner == line, jnp.logical_or(across == 1, across == inner - 1)
+        )
+
+    def count(flag):
+        return flag.astype(jnp.int32)
+
+    side_higher = count(place < inner - 1)
+    turn_higher = count(jnp.logical_and(place == inner - 1, tile < n_tile - 1))
+    if inner > 2:
+        side_higher = side_higher + count(place == 0)
+
+    def signal(semaphore, to_tile, to_rad):
+        pl.semaphore_signal(semaphore, inc=1, device_id=(to_tile, to_rad), device_id_type=MESH)
+
+    barrier = pltpu.get_barrier_semaphore()
+
+    def announce_tile(d):
+        @pl.when(tile + d < n_tile)
+        def _():
+            signal(barrier, tile + d, rad)
+
+    def announce_rad(d):
+        @pl.when(rad + d < n_rad)
+        def _():
+            signal(barrier, tile, rad + d)
+
+    each(n_tile, announce_tile)
+    each(n_rad, announce_rad)
+
 
     nxt = lax.rem(tile + 1, n_tile)
     prv = lax.rem(tile + n_tile - 1, n_tile)
@@ -158,14 +164,14 @@
     def row_copy(f, way):
         return pltpu.make_async_remote_copy(
             src_ref=f4.at[f, :, strip[way]], dst_ref=edge.at[f, :, strip[way]],
-            send_sem=row_send.at[f, way], recv_sem=row_recv.at[f, way],
+            send_sem=row_send.at[way], recv_sem=row_recv.at[f, way],
             device_id=(partner[way], rad), device_id_type=MESH,
         )
 
     def hop_copy(f, way):
         return pltpu.make_async_remote_copy(
             src_ref=f4.at[f, :, strip[way]], dst_ref=relay.at[f - shared, :, strip[way]],
-            send_sem=row_send.at[f, way], recv_sem=hop_recv.at[f - shared, way],
+            send_sem=row_send.at[way], recv_sem=hop_recv.at[f - shared, way],
             device_id=(via[way], rad), device_id_type=MESH,
         )
 
@@ -179,11 +185,12 @@
     shared = half - 1
     relayed = [*range(half, F), shared] if relays else []
     def by_relay(f, way, source):
-        wraps = source == n_tile - 1
-        if f == shared and way == 0 and relays:
-            return jnp.logical_and(wraps, lax.rem(rad, MORE) == 0)
-        if f == F - 1 and way == 0 and relays:
-            return jnp.logical_or(wraps, lax.rem(rad, FEWER) != 0)
+        wraps = source == (n_tile - 1, 0)[way]
+        if f == shared and relays:
+            return jnp.logical_and(wraps, MORE[way](rad))
+        if f == F - 1 and relays:
+            lighter = wraps if way else jnp.logical_not(wraps)
+            return jnp.logical_not(jnp.logical_and(lighter, FEWER[way](rad)))
         return jnp.logical_and(tile >= 0, f in relayed and f != shared)
 
     def start_hops(way):
@@ -265,53 +272,72 @@
         def _():
             signal(rad_sem, tile, rad - d)
 
-    each(n_tile, report_tile)
-    each(n_rad, report_rad)
+    report_tile(1)
     start_hops(0)
     start_beside(1, order[:EARLY])
+    for copy in load_small[:3] + load_x2:
+        copy.start()
     start_crossing(whole[:CROSS], 0, nxt < tile)
     start_crossing(whole[:CROSS], 1, prv < tile)
+    if n_tile <= 8:
+        for d in range(n_tile - 1, 1, -1):
+            report_tile(d)
+    else:
+        lax.fori_loop(2, n_tile, lambda d, c: (report_tile(d), c)[1], 0)
+    each(n_rad, report_rad)
 
     @pl.when(has_below)
     def _():
         lvl_down.start()
 
+    for copy in load_small[3:]:
+        copy.start()
+    load_ext.start()
+    for copy in load_small[:3]:
+        copy.wait()
+
+    def fill_taps(span):
+        diff = lax.broadcasted_iota(jnp.int32, (C, T), 0) - dcol[...]
+        rows = drow[...]
+        for r in span:
+            weights = []
+            for b in range(4):
+                w = jnp.zeros((1, T), jnp.float32)
+                for a in range(4):
+                    w = jnp.where(rows + a == r, lagrange[4 * a + b : 4 * a + b + 1, :], w)
+                weights.append(w)
+            g = jnp.where(diff == 0, weights[0], 0.0)
+            for b in range(1, 4):
+                g = jnp.where(diff == b, weights[b], g)
+            taps[0, r], taps[1, r] = split(g)
+
+    fill_taps(range(HEAD))
     await_signals(side_sem, side_higher)
     start_hops(1)
     start_beside(0, order[:EARLY])
+    fill_taps(range(HEAD, R))
     await_signals(turn_sem, turn_higher)
-    start_crossing(whole[:CROSS], 0, nxt > tile)
+    start_crossing(whole[:CROSS_UP], 0, nxt > tile)
     await_signals(rad_sem, n_rad - 1 - rad)
 
     @pl.when(has_above)
     def _():
         lvl_up.start()
 
-    for copy in load_small:
+    for copy in load_x2:
+        copy.wait()
+    values = jnp.zeros((V, T), jnp.float32)
+    for r in range(R):
+        gh = taps[0, r]
+        gl = taps[1, r]
+        xh, xl = split(
+            jnp.concatenate([x2[h, pl.ds(r, V, stride=R), :] for h in range(halves)], axis=1)
+        )
+        values = values + (dot(xh, gh) + (dot(xl, gh) + dot(xh, gl)))
+
+    for copy in load_small[3:]:
         copy.wait()
     opsum[...] = jnp.sum(opacity[...], axis=0)
-    for copy in load_x2:
-        copy.wait()
-
-    values = jnp.zeros((V, T), jnp.float32)
-    diff = lax.broadcasted_iota(jnp.int32, (C, T), 0) - dcol[...]
-    rows = drow[...]
-    for r in range(R):
-        weights = []
-        for b in range(4):
-            w = jnp.zeros((1, T), jnp.float32)
-            for a in range(4):
-                w = jnp.where(rows + a == r, lagrange[4 * a + b : 4 * a + b + 1, :], w)
-            weights.append(w)
-        g = jnp.where(diff == 0, weights[0], 0.0)
-        for b in range(1, 4):
-            g = jnp.where(diff == b, weights[b], g)
-        gh, gl = split(g)
-        xh, xl = split(
-            jnp.concatenate([x2[h, pl.ds(r, V, stride=R), :] for h in range(halves)], axis=1)
-        )
-        values = values + (dot(xh, gh) + (dot(xl, gh) + dot(xh, gl)))
-
     target = ttile[...]
     kinds = max(16, n_tile)
     hot = (lax.broadcasted_iota(jnp.int32, (kinds, T), 0) == target).astype(jnp.float32)
@@ -355,7 +381,7 @@
     def a2a_copy(d):
         return pltpu.make_async_remote_copy(
             src_ref=chunks.at[d, used], dst_ref=inc.at[d, used],
-            send_sem=a2a_send.at[d], recv_sem=a2a_recv.at[d],
+            send_sem=a2a_send, recv_sem=a2a_recv.at[d],
             device_id=(lax.rem(tile + d, n_tile), rad), device_id_type=MESH,
         )
 
@@ -376,7 +402,8 @@
         each(n_tile, lambda d: a2a_copy(d).start())
     for copy in op_copies:
         copy.start()
-    start_crossing(whole[CROSS:], 0, tile >= 0)
+    start_crossing(whole[CROSS_UP:], 0, nxt > tile)
+    start_crossing(whole[CROSS:], 0, nxt < tile)
     start_crossing(whole[CROSS:], 1, tile >= 0)
     start_beside(1, order[EARLY:])
     start_beside(0, order[EARLY:])
@@ -446,12 +473,55 @@
 
     lax.fori_loop(0, L, cool, above)
 
-    for d in range(1, n_tile):
-        a2a_copy(d).wait_recv()
+    row = lax.broadcasted_iota(jnp.int32, (STEP, R, C), 1)
+
+    def await_rows(f):
+        @pl.when(has_prev)
+        def _():
+            row_copy(f, 0).wait_recv()
+
+        @pl.when(has_next)
+        def _():
+            row_copy(f, 1).wait_recv()
+
+    def received(f, l):
+        at = pl.ds(pl.multiple_of((f * L + l) * R, STEP * R), STEP * R)
+        return jnp.concatenate(
+            [ghost[h, at, :].reshape(STEP, R, LANES) for h in range(halves)], axis=2
+        )
+
+    def row_part(f, finish, i, carry):
+        l = i * STEP
+        u = ext[f, pl.ds(l + 3, STEP)]
+        speed2 = ext[2, pl.ds(l + 3, STEP)]
+        rim = edge[f, pl.ds(l, STEP)]
+        ups = [pltpu.roll(jnp.where(row < k, rim, u), R - k, 1) for k in (1, 2, 3)]
+        downs = [pltpu.roll(jnp.where(row >= R - k, rim, u), k, 1) for k in (1, 2, 3)]
+        first, second = pair_terms(u, ups, downs)
+        total = acc[f, pl.ds(l, STEP)] + (VISCOSITY * second - speed2 * first)
+        if finish:
+            total = total + COUPLING * (received(f, l) - hits[...] * u)
+            total = u + TIME_STEP * total
+        acc[f, pl.ds(l, STEP)] = total
+        return carry
+
+    def ghost_part(f, i, carry):
+        l = i * STEP
+        u = ext[f, pl.ds(l + 3, STEP)]
+        total = acc[f, pl.ds(l, STEP)] + COUPLING * (received(f, l) - hits[...] * u)
+        acc[f, pl.ds(l, STEP)] = u + TIME_STEP * total
+        return carry
+
+    for f in order[:PRE]:
+        await_rows(f)
+        lax.fori_loop(0, L // STEP, functools.partial(row_part, f, False), 0)
+
     group_of = lax.broadcasted_iota(jnp.int32, (1, LANES), 1) // cap
-    row_marks = []
-    column_marks = []
-    for d0 in range(0, n_tile, pack):
+    row_marks = {}
+    column_marks = {}
+    for d0 in sorted(range(0, n_tile, pack), key=lambda d: abs(2 * d + 1 - n_tile)):
+        for d in range(max(d0, 1), d0 + pack):
+            a2a_copy(d).wait_recv()
         lanes = pl.ds(d0 // pack * LANES, LANES)
         parts = [inc[d0 + j] for j in range(pack)]
         for g in range(pack):
@@ -471,10 +541,10 @@
         for j in range(1, pack):
             row_mark = jnp.where(group_of == j, parts[j][VP : VP + 1], row_mark)
             column_mark = jnp.where(group_of == j, parts[j][VP + 1 : VP + 2], column_mark)
-        row_marks.append(row_mark)
-        column_marks.append(column_mark)
-    row_mark = jnp.concatenate(row_marks, axis=1).astype(jnp.int32)
-    column_mark = jnp.concatenate(column_marks, axis=1).astype(jnp.int32)
+        row_marks[d0] = row_mark
+        column_marks[d0] = column_mark
+    row_mark = jnp.concatenate([row_marks[d] for d in sorted(row_marks)], axis=1).astype(jnp.int32)
+    column_mark = jnp.concatenate([column_marks[d] for d in sorted(column_marks)], axis=1).astype(jnp.int32)
     slots = n_tile * cap
     cell_column = lax.broadcasted_iota(jnp.int32, (C, slots), 0)
     everything = xall[...]
@@ -487,58 +557,49 @@
             ghost[h, pl.ds(r, V, stride=R), :] = total[:, h * LANES : (h + 1) * LANES]
         hits[pl.ds(r, 1), :] = got[2 * V : 2 * V + 1]
 
-    row = lax.broadcasted_iota(jnp.int32, (STEP, R, C), 1)
-
-    for f in order:
-        @pl.when(has_prev)
-        def _():
-            row_copy(f, 0).wait_recv()
-
-        @pl.when(has_next)
-        def _():
-            row_copy(f, 1).wait_recv()
-
-        def row_part(i, carry):
-            l = i * STEP
-            u = ext[f, pl.ds(l + 3, STEP)]
-            speed2 = ext[2, pl.ds(l + 3, STEP)]
-            at = pl.ds(pl.multiple_of((f * L + l) * R, STEP * R), STEP * R)
-            rim = edge[f, pl.ds(l, STEP)]
-            arrived = jnp.concatenate(
-                [ghost[h, at, :].reshape(STEP, R, LANES) for h in range(halves)], axis=2
-            )
-            ups = [pltpu.roll(jnp.where(row < k, rim, u), R - k, 1) for k in (1, 2, 3)]
-            downs = [pltpu.roll(jnp.where(row >= R - k, rim, u), k, 1) for k in (1, 2, 3)]
-            first, second = pair_terms(u, ups, downs)
-            total = acc[f, pl.ds(l, STEP)] + (VISCOSITY * second - speed2 * first)
-            total = total + COUPLING * (arrived - hits[...] * u)
-            acc[f, pl.ds(l, STEP)] = u + TIME_STEP * total
-            return carry
-
-        lax.fori_loop(0, L // STEP, row_part, 0)
-
-    @pl.when(has_above)
-    def _():
-        lvl_up.wait_send()
-
-    @pl.when(has_below)
-    def _():
-        lvl_down.wait_send()
-
-    for copy in op_copies:
-        copy.wait_send()
-    for d in range(1, n_tile):
-        a2a_copy(d).wait_send()
-    for f in range(F):
+
+    def drain():
+        @pl.when(has_above)
+        def _():
+            lvl_up.wait_send()
+
+        @pl.when(has_below)
+        def _():
+            lvl_down.wait_send()
+
+        for copy in op_copies:
+            copy.wait_send()
+        for f in relayed:
+            for way in range(2):
+                @pl.when(jnp.logical_and(forwards[way], by_relay(f, way, origin[way])))
+                def _():
+                    forward_copy(f, way).wait_send()
+
+    def drain_rest():
+        pltpu.make_async_remote_copy(
+            src_ref=chunks.at[pl.ds(1, n_tile - 1), used],
+            dst_ref=inc.at[pl.ds(1, n_tile - 1), used],
+            send_sem=a2a_send, recv_sem=a2a_recv.at[1],
+            device_id=(nxt, rad), device_id_type=MESH,
+        ).wait_send()
         for way in range(2):
             @pl.when(sends[way])
             def _():
-                row_copy(f, way).wait_send()
-
-            if f in relayed:
-                @pl.when(jnp.logical_and(forwards[way], by_relay(f, way, origin[way])))
-                def _():
-                    forward_copy(f, way).wait_send()
+                pltpu.make_async_remote_copy(
+                    src_ref=f4.at[:, :, strip[way]], dst_ref=edge.at[:, :, strip[way]],
+                    send_sem=row_send.at[way], recv_sem=row_recv.at[0, way],
+                    device_id=(partner[way], rad), device_id_type=MESH,
+                ).wait_send()
+
+    for f in order[:PRE]:
+        lax.fori_loop(0, L // STEP, functools.partial(ghost_part, f), 0)
+    for f in order[PRE:]:
+        if f == order[-1]:
+            drain()
+        await_rows(f)
+        lax.fori_loop(0, L // STEP, functools.partial(row_part, f, True), 0)
+
+    drain_rest()
 
 
 def shards(n_tile, n_rad, inner, fields, opacity, donor_row, donor_column, target_tile, target_cell, lagrange):
@@ -560,6 +621,7 @@
         scratch_shapes=[
             pltpu.VMEM((C // LANES, V * R, LANES), f32),
             pltpu.VMEM((F, L + 6, R, C), f32),
+            pltpu.VMEM((2, R, C, T), jnp.bfloat16),
             pltpu.VMEM((F, L, R, C), f32),
             pltpu.VMEM((F - F // 2 + 1, L, R, C), f32),
             pltpu.VMEM((C // LANES, V * R, LANES), f32),
@@ -584,13 +646,13 @@
             pltpu.SemaphoreType.REGULAR,
             dma((2,)),
             dma((2,)),
-            dma((F, 2)),
+            dma((2,)),
             dma((F, 2)),
             dma((F - F // 2 + 1, 2)),
             dma((F - F // 2 + 1, 2)),
             dma((n_rad - 1,)),
             dma((n_rad - 1,)),
-            dma((n_tile,)),
+            dma(()),
             dma((n_tile,)),
         ],
         compiler_params=pltpu.CompilerParams(

time: 30.4 us -> 29.7 us (0.977)
  the two profiles are of different devices: /device:TPU:18 before, /device:TPU:0 now
where the time goes in v4:
time: 29.7 us; the launch traced here: 29.1 us
  Pallas kernels  28 us (94%)
  local copies, waits for them, and re-layouts  1.15 us (4%)
    pallas_call x1, Pallas kernels, shards(): pl.pallas_call(functools.partial(kernel, n_tile, n_rad, inner, cap), out_...  28 us
    unnamed x1, local copies, waits for them, and re-layouts  1.15 us

profile of v4, /device:TPU:0, one launch (start us, length us, event | category | flops | bytes accessed | tf_op | source)
XLA Modules:
  0.0 29.1 jit_solution(12085768641026019271)
XLA Ops:
  0.0 28.0 %shard_map.73 = f32[8,24,8,256]{3,2,1,0:T(8,128)S(1)} custom-call(f32[8,24,8,256]{3,2,1,0:T(8,128)} %f4.1, f32[1536,256]{1,0:T(8,128)} %bitcast.5, f32[24,8,256]{2,1,0:T(8,128)} %opacity_in.1, s32[1,256]{1,0:T(1,128)} %bitcast.6, s32[1,256]{1,0:T(1,128)} %bitcast.7, s32[1,256]{1,0:T(1,128)} %bitcast.8, s32[1,256]{1,0:T(1,128)} %bitcast.9, f32[16,256]{1,0:T(8,128)} %lagrange_in.1), custom_call_target="tpu_custom_call" | custom-call | tf_op jit(solution)/shard_map/pallas_call | solution.py:616
  28.0 1.1 %copy.9 = f32[8,24,8,256]{3,2,1,0:T(8,128)} copy(f32[8,24,8,256]{3,2,1,0:T(8,128)S(1)} %shard_map.73) | data formatting | bytes 3145728

commit v5 on v4

--- a/solution.py
+++ b/solution.py
@@ -14,24 +14,22 @@
 MESH = pl.DeviceIdType.MESH
 LANES = 128
 EVEN = lambda r: lax.rem(r, 2) == 0
-ODD = lambda r: lax.rem(r, 2) == 1
-ALL = lambda r: r >= 0
 NONE = lambda r: r < 0
-LOW = lambda r: r < 2
-ZERO = lambda r: r == 0
 VMEM_LIMIT = 32 << 20
 STEP = 4
-EARLY = 3
+EARLY = 4
 CROSS = 2
-PRE = 3
+PRE = 4
 HEAD = 0
 CROSS_UP = 2
 MORE = (EVEN, NONE)
-FEWER = (EVEN, NONE)
+FEWER = (NONE, NONE)
 SOON = 2
 ORDER = (0, 1, 4, 5, 6, 2, 3, 7)
 FIRST = 1
 NT = (((1,), (1,)), ((), ()))
+SPREAD = [TIME_STEP * VISCOSITY * w / 180.0 for w in (270.0, -27.0, 2.0)]
+SLOPE = [TIME_STEP * w / 60.0 for w in (45.0, -9.0, 1.0)]
 
 
 def in_hbm(x):
@@ -337,7 +335,6 @@
 
     for copy in load_small[3:]:
         copy.wait()
-    opsum[...] = jnp.sum(opacity[...], axis=0)
     target = ttile[...]
     kinds = max(16, n_tile)
     hot = (lax.broadcasted_iota(jnp.int32, (kinds, T), 0) == target).astype(jnp.float32)
@@ -373,9 +370,6 @@
         for f in relayed[:SOON]:
             forward(f)
 
-    picked, marks = chunk(0)
-    inc[0, pl.ds(0, VP)] = picked
-    inc[0, pl.ds(VP, 8)] = marks
     used = pl.ds(0, VP + 2)
 
     def a2a_copy(d):
@@ -400,13 +394,17 @@
     else:
         each(n_tile, fill_chunk)
         each(n_tile, lambda d: a2a_copy(d).start())
-    for copy in op_copies:
-        copy.start()
+    opsum[...] = jnp.sum(opacity[...], axis=0)
     start_crossing(whole[CROSS_UP:], 0, nxt > tile)
     start_crossing(whole[CROSS:], 0, nxt < tile)
     start_crossing(whole[CROSS:], 1, tile >= 0)
     start_beside(1, order[EARLY:])
     start_beside(0, order[EARLY:])
+    picked, marks = chunk(0)
+    inc[0, pl.ds(0, VP)] = picked
+    inc[0, pl.ds(VP, 8)] = marks
+    for copy in op_copies:
+        copy.start()
 
     load_ext.wait()
     zeros3 = jnp.zeros((F, 3, R, C), jnp.float32)
@@ -490,18 +488,23 @@
             [ghost[h, at, :].reshape(STEP, R, LANES) for h in range(halves)], axis=2
         )
 
-    def row_part(f, finish, i, carry):
+    def row_part(f, keep, i, carry):
         l = i * STEP
         u = ext[f, pl.ds(l + 3, STEP)]
         speed2 = ext[2, pl.ds(l + 3, STEP)]
         rim = edge[f, pl.ds(l, STEP)]
         ups = [pltpu.roll(jnp.where(row < k, rim, u), R - k, 1) for k in (1, 2, 3)]
         downs = [pltpu.roll(jnp.where(row >= R - k, rim, u), k, 1) for k in (1, 2, 3)]
-        first, second = pair_terms(u, ups, downs)
-        total = acc[f, pl.ds(l, STEP)] + (VISCOSITY * second - speed2 * first)
-        if finish:
-            total = total + COUPLING * (received(f, l) - hits[...] * u)
-            total = u + TIME_STEP * total
+        if keep is not None:
+            sums = [a + b for a, b in zip(ups, downs)]
+            jumps = [a - b for a, b in zip(ups, downs)]
+            spread = sum(w * a for w, a in zip(SPREAD, sums))
+            slope = sum(w * a for w, a in zip(SLOPE, jumps))
+            total = TIME_STEP * (acc[f, pl.ds(l, STEP)] + COUPLING * received(f, l))
+            total = total + keep * u + (spread - speed2 * slope)
+        else:
+            first, second = pair_terms(u, ups, downs)
+            total = acc[f, pl.ds(l, STEP)] + (VISCOSITY * second - speed2 * first)
         acc[f, pl.ds(l, STEP)] = total
         return carry
 
@@ -514,7 +517,7 @@
 
     for f in order[:PRE]:
         await_rows(f)
-        lax.fori_loop(0, L // STEP, functools.partial(row_part, f, False), 0)
+        lax.fori_loop(0, L // STEP, functools.partial(row_part, f, None), 0)
 
     group_of = lax.broadcasted_iota(jnp.int32, (1, LANES), 1) // cap
     row_marks = {}
@@ -593,11 +596,12 @@
 
     for f in order[:PRE]:
         lax.fori_loop(0, L // STEP, functools.partial(ghost_part, f), 0)
+    keep = (1.0 + TIME_STEP * VISCOSITY * (-490.0 / 180.0)) - TIME_STEP * COUPLING * hits[...]
     for f in order[PRE:]:
         if f == order[-1]:
             drain()
         await_rows(f)
-        lax.fori_loop(0, L // STEP, functools.partial(row_part, f, True), 0)
+        lax.fori_loop(0, L // STEP, functools.partial(row_part, f, keep), 0)
 
     drain_rest()
 

time: 29.7 us -> 29.5 us (level)
  no operation moved by 1% of the time
where the time goes in v5:
time: 29.5 us; the launch traced here: 29.1 us
  Pallas kernels  27.9 us (95%)
  local copies, waits for them, and re-layouts  1.15 us (4%)
    pallas_call x1, Pallas kernels, shards(): pl.pallas_call(functools.partial(kernel, n_tile, n_rad, inner, cap), out_...  27.9 us
    unnamed x1, local copies, waits for them, and re-layouts  1.15 us

profile of v5, /device:TPU:0, one launch (start us, length us, event | category | flops | bytes accessed | tf_op | source)
XLA Modules:
  0.0 29.1 jit_solution(9231638036818960068)
XLA Ops:
  0.0 27.9 %shard_map.73 = f32[8,24,8,256]{3,2,1,0:T(8,128)S(1)} custom-call(f32[8,24,8,256]{3,2,1,0:T(8,128)} %f4.1, f32[1536,256]{1,0:T(8,128)} %bitcast.5, f32[24,8,256]{2,1,0:T(8,128)} %opacity_in.1, s32[1,256]{1,0:T(1,128)} %bitcast.6, s32[1,256]{1,0:T(1,128)} %bitcast.7, s32[1,256]{1,0:T(1,128)} %bitcast.8, s32[1,256]{1,0:T(1,128)} %bitcast.9, f32[16,256]{1,0:T(8,128)} %lagrange_in.1), custom_call_target="tpu_custom_call" | custom-call | tf_op jit(solution)/shard_map/pallas_call | solution.py:620
  27.9 1.1 %copy.9 = f32[8,24,8,256]{3,2,1,0:T(8,128)} copy(f32[8,24,8,256]{3,2,1,0:T(8,128)S(1)} %shard_map.73) | data formatting | bytes 3145728

commit v6 on v5

--- a/solution.py
+++ b/solution.py
@@ -16,7 +16,7 @@
 EVEN = lambda r: lax.rem(r, 2) == 0
 NONE = lambda r: r < 0
 VMEM_LIMIT = 32 << 20
-STEP = 4
+STEP = 8
 EARLY = 4
 CROSS = 2
 PRE = 4
@@ -26,7 +26,7 @@
 FEWER = (NONE, NONE)
 SOON = 2
 ORDER = (0, 1, 4, 5, 6, 2, 3, 7)
-FIRST = 1
+FIRST = 0
 NT = (((1,), (1,)), ((), ()))
 SPREAD = [TIME_STEP * VISCOSITY * w / 180.0 for w in (270.0, -27.0, 2.0)]
 SLOPE = [TIME_STEP * w / 60.0 for w in (45.0, -9.0, 1.0)]

time: 29.5 us -> 29.5 us (level)
  no operation moved by 1% of the time
where the time goes in v6:
time: 29.5 us; the launch traced here: 29.1 us
  Pallas kernels  27.9 us (95%)
  local copies, waits for them, and re-layouts  1.15 us (4%)
    pallas_call x1, Pallas kernels, shards(): pl.pallas_call(functools.partial(kernel, n_tile, n_rad, inner, cap), out_...  27.9 us
    unnamed x1, local copies, waits for them, and re-layouts  1.15 us

profile of v6, /device:TPU:0, one launch (start us, length us, event | category | flops | bytes accessed | tf_op | source)
XLA Modules:
  0.0 29.1 jit_solution(7148651325817536314)
XLA Ops:
  0.0 27.9 %shard_map.73 = f32[8,24,8,256]{3,2,1,0:T(8,128)S(1)} custom-call(f32[8,24,8,256]{3,2,1,0:T(8,128)} %f4.1, f32[1536,256]{1,0:T(8,128)} %bitcast.5, f32[24,8,256]{2,1,0:T(8,128)} %opacity_in.1, s32[1,256]{1,0:T(1,128)} %bitcast.6, s32[1,256]{1,0:T(1,128)} %bitcast.7, s32[1,256]{1,0:T(1,128)} %bitcast.8, s32[1,256]{1,0:T(1,128)} %bitcast.9, f32[16,256]{1,0:T(8,128)} %lagrange_in.1), custom_call_target="tpu_custom_call" | custom-call | tf_op jit(solution)/shard_map/pallas_call | solution.py:620
  27.9 1.1 %copy.9 = f32[8,24,8,256]{3,2,1,0:T(8,128)} copy(f32[8,24,8,256]{3,2,1,0:T(8,128)S(1)} %shard_map.73) | data formatting | bytes 3145728

commit v7 on v6

--- a/solution.py
+++ b/solution.py
@@ -20,7 +20,7 @@
 EARLY = 4
 CROSS = 2
 PRE = 4
-HEAD = 0
+HEAD = 1
 CROSS_UP = 2
 MORE = (EVEN, NONE)
 FEWER = (NONE, NONE)

time: 29.5 us -> 29.5 us (level)
  no operation moved by 1% of the time
where the time goes in v7:
time: 29.5 us; the launch traced here: 29.1 us
  Pallas kernels  27.9 us (95%)
  local copies, waits for them, and re-layouts  1.15 us (4%)
    pallas_call x1, Pallas kernels, shards(): pl.pallas_call(functools.partial(kernel, n_tile, n_rad, inner, cap), out_...  27.9 us
    unnamed x1, local copies, waits for them, and re-layouts  1.15 us

profile of v7, /device:TPU:0, one launch (start us, length us, event | category | flops | bytes accessed | tf_op | source)
XLA Modules:
  0.0 29.1 jit_solution(17184892068230453889)
XLA Ops:
  0.0 27.9 %shard_map.73 = f32[8,24,8,256]{3,2,1,0:T(8,128)S(1)} custom-call(f32[8,24,8,256]{3,2,1,0:T(8,128)} %f4.1, f32[1536,256]{1,0:T(8,128)} %bitcast.5, f32[24,8,256]{2,1,0:T(8,128)} %opacity_in.1, s32[1,256]{1,0:T(1,128)} %bitcast.6, s32[1,256]{1,0:T(1,128)} %bitcast.7, s32[1,256]{1,0:T(1,128)} %bitcast.8, s32[1,256]{1,0:T(1,128)} %bitcast.9, f32[16,256]{1,0:T(8,128)} %lagrange_in.1), custom_call_target="tpu_custom_call" | custom-call | tf_op jit(solution)/shard_map/pallas_call | solution.py:620
  27.9 1.1 %copy.9 = f32[8,24,8,256]{3,2,1,0:T(8,128)} copy(f32[8,24,8,256]{3,2,1,0:T(8,128)S(1)} %shard_map.73) | data formatting | bytes 3145728
